TPU v7x, 32 devices: a whole 2x2x4 slice. The times are simulated.
32 devices in a mesh: groups: 2 (over y), seq: 4 (over z), head: 2 (over x), sub: 2 (over core).
Axes of the slice: x: 2, y: 2, z: 4, core: 2. Of those that a mesh axis runs over, the one named last changes fastest.
Arguments:
- hidden_states: bfloat16 [8192, 8192], P(('groups', 'seq', 'sub'), 'head'), parts along dimension 0, may hold values from -42 to 42
- key_projection_weight: bfloat16 [8192, 1024], P(('seq', 'sub'), 'head'), may hold values from -0.0625 to 0.0625
- value_projection_weight: bfloat16 [8192, 1024], P(('seq', 'sub'), 'head'), may hold values from -0.0625 to 0.0625
- head_basis_matrix: float32 [8, 128, 64], P('head'), may hold values from -0.5 to 0.5
- slot_token: int32 [8192], P(('groups', 'seq', 'sub')), parts along dimension 0, may hold values from 0 to 4095, as said below
Outputs:
- compressed_keys: bfloat16 [8192, 512], P(('groups', 'seq', 'sub'), 'head'), parts along dimension 0
- value_cache: bfloat16 [8192, 1024], P(('groups', 'seq', 'sub'), 'head'), parts along dimension 0
There are 2 independent parts, one for each index of `groups`. A program takes and returns all parts, laid end to end along the dimension named above; an argument that names none is the same for every part. Nothing has to cross between parts.
Inputs may be any that keep to these rules, and one draw needn't show every extreme that they name: `slot_token`: A permutation of the 4096 token positions. Each aligned block of 512 rows holds exactly 64 positions of each aligned block of 512 positions.
All inputs are finite; a program needn't handle non-finite values.
Results may differ from a plain program's by a relative error of at most 0.0055.
Values may be sent and summed in bfloat16 or wider, within the bound.
No kernel may reach another device: no remote copies, remote signals or barrier semaphores. Data moves between devices by JAX's collectives and lax.ppermute only.
A program may use at most 64 MiB of HBM per device.

v0:
```python
import jax
import jax.numpy as jnp
from jax import lax
from jax.sharding import PartitionSpec as P

ridge_share = 0.05


def covariance_sum(decode_key_cache, heads_here, head_dim, token_total):
    per_head_keys = decode_key_cache.reshape(decode_key_cache.shape[0], heads_here, head_dim)
    local_terms = jnp.einsum(
        "thi,thj->hij", per_head_keys, per_head_keys, preferred_element_type=jnp.float32
    )
    summed = lax.psum(local_terms, ("seq", "sub"))
    return summed / token_total


def per_device(
    hidden_states, key_projection_weight, value_projection_weight, head_basis_matrix, slot_token
):
    tokens_here = hidden_states.shape[0]
    seq_count = lax.axis_size("seq")
    core_count = lax.axis_size("sub")
    device_count = seq_count * core_count
    token_total = tokens_here * device_count
    heads_here = head_basis_matrix.shape[0]
    head_dim = head_basis_matrix.shape[1]
    rank_dim = head_basis_matrix.shape[2]
    gathered = lax.all_gather(hidden_states, "head", axis=1, tiled=True)
    key_sums = jnp.dot(
        gathered,
        lax.all_gather(key_projection_weight, ("seq", "sub"), axis=0, tiled=True),
        preferred_element_type=jnp.float32,
    )
    value_sums = jnp.dot(
        gathered,
        lax.all_gather(value_projection_weight, ("seq", "sub"), axis=0, tiled=True),
        preferred_element_type=jnp.float32,
    )
    decode_key_cache = key_sums.astype(jnp.bfloat16)
    moments = covariance_sum(decode_key_cache, heads_here, head_dim, token_total)
    value_cache = value_sums.astype(jnp.bfloat16)
    trace_vals = jnp.trace(moments, axis1=1, axis2=2)
    identity = jnp.eye(head_dim, dtype=jnp.float32)
    regular = moments + (ridge_share * trace_vals / head_dim)[:, None, None] * identity
    factor = jnp.linalg.cholesky(regular)
    by_head = jnp.transpose(
        decode_key_cache.astype(jnp.float32).reshape(tokens_here, heads_here, head_dim), (1, 0, 2)
    )
    whitened = lax.linalg.triangular_solve(
        factor, by_head, left_side=False, lower=True, transpose_a=True
    )
    basis_coefficients = jnp.einsum(
        "htd,hdr->htr", whitened, head_basis_matrix, precision=lax.Precision.HIGHEST
    )
    compressed = (
        jnp.transpose(basis_coefficients, (1, 0, 2))
        .reshape(tokens_here, heads_here * rank_dim)
        .astype(jnp.bfloat16)
    )
    row_order = jnp.argsort(slot_token)
    wanted = slot_token[row_order]
    asked = lax.all_to_all(wanted, ("seq", "sub"), split_axis=0, concat_axis=0, tiled=True)
    local_rows = asked % tokens_here
    got_coeffs, got_values = (
        lax.all_to_all(
            compressed[local_rows], ("seq", "sub"), split_axis=0, concat_axis=0, tiled=True
        ),
        lax.all_to_all(
            value_cache[local_rows], ("seq", "sub"), split_axis=0, concat_axis=0, tiled=True
        ),
    )
    inverse = jnp.argsort(row_order)
    return (got_coeffs[inverse], got_values[inverse])


def solution(mesh):
    return jax.shard_map(
        per_device,
        mesh=mesh,
        in_specs=(
            P(("groups", "seq", "sub"), "head"),
            P(("seq", "sub"), "head"),
            P(("seq", "sub"), "head"),
            P("head", None, None),
            P(("groups", "seq", "sub")),
        ),
        out_specs=(P(("groups", "seq", "sub"), "head"), P(("groups", "seq", "sub"), "head")),
        check_vma=False,
    )
```

profile of v0, /device:TPU:0, one launch (start us, length us, event | category | flops | bytes accessed | tf_op | source)
XLA Modules:
  0.0 405.3 jit_solution(3034889648175689121)
XLA Ops:
  7.2 0.0 copy-start
  7.2 0.0 all-gather.4.cloned.1.call-start
  7.2 0.7 all-gather.4.cloned.1.call-update
  7.9 0.0 all-gather.6.cloned.1.call-start
  8.0 0.7 all-gather.6.cloned.1.call-update
  8.7 0.0 copy-start.1
  8.7 0.0 all-reduce.2.cloned.1.call-start
  8.7 107.6 %all-gather.4.cloned.1.call-done = bf16[512,8192]{1,0:T(8,128)(2,1)} async-done(((bf16[512,4096]{1,0:T(8,128)(2,1)}), bf16[512,8192]{1,0:T(8,128)(2,1)}) %all-gather.4.cloned.1.call-update) | async-done | bytes 8388624 | tf_op jit(solution)/shard_map/all_gather | solution.py:29
  116.3 83.7 %all-gather.6.cloned.1.call-done = bf16[8192,512]{1,0:T(8,128)(2,1)} async-done(((bf16[1024,512]{1,0:T(8,128)(2,1)}), bf16[8192,512]{1,0:T(8,128)(2,1)}) %all-gather.6.cloned.1.call-update) | async-done | bytes 8388624 | tf_op jit(solution)/shard_map/all_gather | solution.py:32
  200.0 10.3 %convolution_convert_fusion.1 = bf16[512,512]{0,1:T(8,128)(2,1)S(1)} fusion(bf16[512,8192]{1,0:T(8,128)(2,1)} %all-gather.4.cloned.1.call-done, bf16[8192,512]{1,0:T(8,128)(2,1)} %all-gather.6.cloned.1.call-done), kind=kOutput, calls=%fused_computation.6 | convolution fusion | flops 4295229440 | bytes 17301504 | tf_op jit(solution)/shard_map/dot_general | solution.py:30
  210.3 1.0 fusion.6
  211.3 0.0 all-reduce.2.cloned.1.call-update
  211.3 0.0 all-gather.8.cloned.1.call-start
  211.4 0.5 all-gather.8.cloned.1.call-update
  211.9 0.0 copy-done.1
  211.9 3.8 sort.31
  215.7 3.5 gather_fusion
  219.2 0.7 all_to_all.24
  219.9 3.5 all-to-all-start
  223.4 5.2 %all-to-all-done = s32[8,64,1]{1,2,0:T(1,128)S(1)} async-done(((s32[8,64,1]{1,2,0:T(1,128)}), s32[8,64,1]{1,2,0:T(1,128)S(1)}, u32[]{:S(2)}, u32[]{:S(2)}) %all-to-all-start) | async-done | bytes 2080 | tf_op jit(solution)/shard_map/all_to_all | solution.py:63
  228.6 0.5 broadcast.144
  229.1 0.7 reduce.9
  229.8 0.1 all_to_all.26
  229.9 0.3 copy.19
  230.2 34.9 %all-reduce.2.cloned.1.call-done = f32[4,128,128]{2,1,0:T(8,128)} async-done(((f32[4,128,128]{2,1,0:T(8,128)}), f32[4,128,128]{2,1,0:T(8,128)}) %all-reduce.2.cloned.1.call-update) | async-done | bytes 262160 | tf_op jit(solution)/shard_map/psum | solution.py:14
  265.1 1.1 select_reduce_fusion.1
  266.1 1.0 multiply_add_fusion
  267.2 0.1 copy.21
  267.3 1.1 fusion.3
  268.4 46.9 %custom-call.7 = f32[4,128,128]{2,1,0:T(8,128)S(1)} custom-call(f32[4,128,128]{2,1,0:T(8,128)S(1)} %fusion.3), custom_call_target="Cholesky" | custom-call | tf_op jit(solution)/shard_map/jit(cholesky)/cholesky | solution.py:46
  315.3 0.1 compare_reduce_fusion
  315.5 0.1 select_bitcast_fusion
  315.6 39.3 %custom-call.8 = f32[4,1,128,128]{2,3,1,0:T(8,128)S(1)} custom-call(f32[4,1,128,128]{3,2,1,0:T(8,128)S(1)} %select_bitcast_fusion), custom_call_target="InvertDiagBlocksLowerTriangular" | custom-call | tf_op jit(solution)/shard_map/triangular_solve | solution.py:50
  354.9 0.6 fusion
  355.5 0.0 copy-done
  355.5 1.3 convolution_convert_fusion.2
  356.7 0.1 copy.24
  356.9 2.6 gather_fusion.1
  359.5 3.6 all-to-all-start.1
  363.1 0.0 all-gather.8.cloned.1.call-done
  363.1 10.2 %convolution_convert_fusion = bf16[512,512]{1,0:T(8,128)(2,1)S(1)} fusion(bf16[512,8192]{1,0:T(8,128)(2,1)} %all-gather.4.cloned.1.call-done, bf16[8192,512]{1,0:T(8,128)(2,1)} %all-gather.8.cloned.1.call-done), kind=kOutput, calls=%fused_computation.5 | convolution fusion | flops 4295229440 | bytes 17301504 | tf_op jit(solution)/shard_map/dot_general | solution.py:35
  373.4 2.6 gather_fusion.3
  376.0 0.0 all-to-all-done.1
  376.0 4.8 %all-to-all-start.2 = ((bf16[8,64,512]{2,1,0:T(8,128)(2,1)}), bf16[8,64,512]{2,1,0:T(8,128)(2,1)S(1)}, u32[]{:S(2)}, u32[]{:S(2)}) async-start(bf16[8,64,512]{2,1,0:T(8,128)(2,1)} %bitcast.11), calls=%async_computation.2 | async-start | bytes 1048576 | tf_op jit(solution)/shard_map/all_to_all | solution.py:69
  380.8 3.8 sort.32
  384.6 2.6 gather_fusion.2
  387.2 9.0 %all-to-all-done.2 = bf16[8,64,512]{2,1,0:T(8,128)(2,1)S(1)} async-done(((bf16[8,64,512]{2,1,0:T(8,128)(2,1)}), bf16[8,64,512]{2,1,0:T(8,128)(2,1)S(1)}, u32[]{:S(2)}, u32[]{:S(2)}) %all-to-all-start.2) | async-done | bytes 524320 | tf_op jit(solution)/shard_map/all_to_all | solution.py:69
  396.2 2.6 gather_fusion.4
  (13 shorter events, 0.1 us)
Async XLA Ops:
  7.2 348.3 %copy-start = (f32[4,128,64]{1,2,0:T(8,128)S(1)}, f32[4,128,64]{1,2,0:T(8,128)}, u32[]{:S(2)}) copy-start(f32[4,128,64]{1,2,0:T(8,128)} %param.8) | copy-start | bytes 393220
  7.2 109.1 %all-gather.4.cloned.1.call-start = ((), (), s32[]{:S(2)}) async-start(), calls=%async_computation.3 | async-start | bytes 12582912 | tf_op jit(solution)/shard_map/all_gather | solution.py:29
  7.9 192.1 %all-gather.6.cloned.1.call-start = ((), (), s32[]{:S(2)}) async-start(), calls=%async_computation.4 | async-start | bytes 9437184 | tf_op jit(solution)/shard_map/all_gather | solution.py:32
  8.7 203.2 %copy-start.1 = (s32[512]{0:T(512)S(1)}, s32[512]{0:T(512)}, u32[]{:S(2)}) copy-start(s32[512]{0:T(512)} %param.9) | copy-start | bytes 6148
  8.7 256.4 %all-reduce.2.cloned.1.call-start = ((), (), s32[]{:S(2)}) async-start(), calls=%async_computation.5 | async-start | bytes 524288 | tf_op jit(solution)/shard_map/psum | solution.py:14
  211.3 151.8 %all-gather.8.cloned.1.call-start = ((), (), s32[]{:S(2)}) async-start(), calls=%async_computation.6 | async-start | bytes 9437184 | tf_op jit(solution)/shard_map/all_gather | solution.py:37
  219.9 8.7 %all-to-all-start = ((s32[8,64,1]{1,2,0:T(1,128)}), s32[8,64,1]{1,2,0:T(1,128)S(1)}, u32[]{:S(2)}, u32[]{:S(2)}) async-start(s32[8,64,1]{1,2,0:T(1,128)} %bitcast.7), calls=%async_computation | async-start | bytes 8192 | tf_op jit(solution)/shard_map/all_to_all | solution.py:63
  359.5 16.6 %all-to-all-start.1 = ((bf16[8,64,256]{2,1,0:T(8,128)(2,1)}), bf16[8,64,256]{2,1,0:T(8,128)(2,1)S(1)}, u32[]{:S(2)}, u32[]{:S(2)}) async-start(bf16[8,64,256]{2,1,0:T(8,128)(2,1)} %bitcast.9), calls=%async_computation.1 | async-start | bytes 524288 | tf_op jit(solution)/shard_map/all_to_all | solution.py:66
  376.0 20.1 %all-to-all-start.2 = ((bf16[8,64,512]{2,1,0:T(8,128)(2,1)}), bf16[8,64,512]{2,1,0:T(8,128)(2,1)S(1)}, u32[]{:S(2)}, u32[]{:S(2)}) async-start(bf16[8,64,512]{2,1,0:T(8,128)(2,1)} %bitcast.11), calls=%async_computation.2 | async-start | bytes 1048576 | tf_op jit(solution)/shard_map/all_to_all | solution.py:69
Sparse Core Ops, SparseCore 0:
  9.6 106.6 all-gather.3
  117.9 82.0 all-gather.5
  211.4 53.5 all-reduce.1
  266.6 81.1 all-gather.7
where the time goes:
time: 406 us; the launch traced here: 405 us
  waiting for transfers between devices  242 us (60%)
  other arithmetic  98 us (24%)
  matrix products  23.4 us (6%)
  local copies, waits for them, and re-layouts  15.7 us (4%)
  between operations  13.9 us (3%)
  starting transfers between devices  12.1 us (3%)
    all_gather x1, waiting for transfers between devices, per_device(): gathered = lax.all_gather(hidden_states, 'head', axis=1, tiled=True)  108 us
    all_gather x1, waiting for transfers between devices, per_device(): lax.all_gather(key_projection_weight, ('seq', 'sub'), axis=0, tiled=True)  83.7 us
    another operation x4, other arithmetic, per_device(): factor = jnp.linalg.cholesky(regular)  47.1 us
    another operation x3, other arithmetic, per_device(): lax.linalg.triangular_solve(factor, by_head, left_side=False, lower=True,...  39.4 us
    psum x1, waiting for transfers between devices, covariance_sum(): summed = lax.psum(local_terms, ('seq', 'sub'))  34.9 us
    dot_general x1, matrix products, per_device(): jnp.dot(gathered, lax.all_gather(key_projection_weight, ('seq', 'sub'), a...  10.3 us
    dot_general x1, matrix products, per_device(): jnp.dot(gathered, lax.all_gather(value_projection_weight, ('seq', 'sub'),...  10.2 us
    all_to_all x1, waiting for transfers between devices, per_device(): lax.all_to_all(value_cache[local_rows], ('seq', 'sub'), split_axis=0, con...  9 us
  transfers between devices with their start and end apart: 7, of which 5 were waited for; matrix products, arithmetic and copies ran while one was open for 30% of the time, Pallas kernels for 0%

commit v1 on v0

--- a/solution.py
+++ b/solution.py
@@ -11,7 +11,7 @@
     local_terms = jnp.einsum(
         "thi,thj->hij", per_head_keys, per_head_keys, preferred_element_type=jnp.float32
     )
-    summed = lax.psum(local_terms, ("seq", "sub"))
+    summed = lax.psum(lax.psum(local_terms, "sub"), "seq")
     return summed / token_total
 
 

time: 406 us -> 470 us (1.16)
  waiting for transfers between devices: 242 us -> 308 us
    all_gather x1, waiting for transfers between devices: 0.02 us -> 83.2 us  [per_device(): lax.all_gather(value_projection_weight, ('seq', 'sub'), axis=0, tiled=True)]
    psum x1 -> x2, waiting for transfers between devices: 34.9 us -> 22.9 us  [covariance_sum(): summed = lax.psum(lax.psum(local_terms, 'sub'), 'seq')]
    all_to_all x1, waiting for transfers between devices: 9 us -> 0.01 us  [per_device(): lax.all_to_all(value_cache[local_rows], ('seq', 'sub'), split_axis=0, con...]
  transfers between devices with their start and end apart: 7 -> 8, of which waited for: 5 -> 6; matrix products, arithmetic and copies ran while one was open for 30% -> 26% of each run, Pallas kernels for 0% -> 0%
where the time goes in v1:
time: 470 us; the launch traced here: 469 us
  waiting for transfers between devices  308 us (66%)
  other arithmetic  98 us (21%)
  matrix products  23.4 us (5%)
  local copies, waits for them, and re-layouts  15.7 us (3%)
  between operations  14 us (3%)
  starting transfers between devices  10.6 us (2%)
    all_gather x1, waiting for transfers between devices, per_device(): gathered = lax.all_gather(hidden_states, 'head', axis=1, tiled=True)  108 us
    all_gather x1, waiting for transfers between devices, per_device(): lax.all_gather(key_projection_weight, ('seq', 'sub'), axis=0, tiled=True)  83.7 us
    all_gather x1, waiting for transfers between devices, per_device(): lax.all_gather(value_projection_weight, ('seq', 'sub'), axis=0, tiled=True)  83.2 us
    another operation x4, other arithmetic, per_device(): factor = jnp.linalg.cholesky(regular)  47.1 us
    another operation x3, other arithmetic, per_device(): lax.linalg.triangular_solve(factor, by_head, left_side=False, lower=True,...  39.4 us
    psum x2, waiting for transfers between devices, covariance_sum(): summed = lax.psum(lax.psum(local_terms, 'sub'), 'seq')  22.9 us
    dot_general x1, matrix products, per_device(): jnp.dot(gathered, lax.all_gather(key_projection_weight, ('seq', 'sub'), a...  10.3 us
    dot_general x1, matrix products, per_device(): jnp.dot(gathered, lax.all_gather(value_projection_weight, ('seq', 'sub'),...  10.2 us
  transfers between devices with their start and end apart: 8, of which 6 were waited for; matrix products, arithmetic and copies ran while one was open for 26% of the time, Pallas kernels for 0%

profile of v1, /device:TPU:0, one launch (start us, length us, event | category | flops | bytes accessed | tf_op | source)
XLA Modules:
  0.0 469.5 jit_solution(11247304850250110608)
XLA Ops:
  7.2 0.0 copy-start
  7.2 0.0 all-gather.4.cloned.1.call-start
  7.2 0.7 all-gather.4.cloned.1.call-update
  7.9 0.0 all-gather.6.cloned.1.call-start
  8.0 0.7 all-gather.6.cloned.1.call-update
  8.7 0.0 all-reduce.3.cloned.1.call-start
  8.7 107.6 %all-gather.4.cloned.1.call-done = bf16[512,8192]{1,0:T(8,128)(2,1)} async-done(((bf16[512,4096]{1,0:T(8,128)(2,1)}), bf16[512,8192]{1,0:T(8,128)(2,1)}) %all-gather.4.cloned.1.call-update) | async-done | bytes 8388624 | tf_op jit(solution)/shard_map/all_gather | solution.py:29
  116.3 83.7 %all-gather.6.cloned.1.call-done = bf16[8192,512]{1,0:T(8,128)(2,1)} async-done(((bf16[1024,512]{1,0:T(8,128)(2,1)}), bf16[8192,512]{1,0:T(8,128)(2,1)}) %all-gather.6.cloned.1.call-update) | async-done | bytes 8388624 | tf_op jit(solution)/shard_map/all_gather | solution.py:32
  200.0 10.3 %convolution_convert_fusion.1 = bf16[512,512]{0,1:T(8,128)(2,1)S(1)} fusion(bf16[512,8192]{1,0:T(8,128)(2,1)} %all-gather.4.cloned.1.call-done, bf16[8192,512]{1,0:T(8,128)(2,1)} %all-gather.6.cloned.1.call-done), kind=kOutput, calls=%fused_computation.6 | convolution fusion | flops 4295229440 | bytes 17301504 | tf_op jit(solution)/shard_map/dot_general | solution.py:30
  210.3 1.0 fusion.6
  211.3 0.0 all-reduce.3.cloned.1.call-update
  211.3 0.0 all-gather.8.cloned.1.call-start
  211.4 0.5 all-gather.8.cloned.1.call-update
  211.9 3.8 sort.31
  215.7 3.5 gather_fusion
  219.2 0.7 all_to_all.24
  219.9 3.3 all-to-all-start
  223.2 0.0 all-reduce.5.cloned.1.call-start
  223.3 5.3 %all-to-all-done = s32[8,64,1]{1,2,0:T(1,128)S(1)} async-done(((s32[8,64,1]{1,2,0:T(1,128)}), s32[8,64,1]{1,2,0:T(1,128)S(1)}, u32[]{:S(2)}, u32[]{:S(2)}) %all-to-all-start) | async-done | bytes 2080 | tf_op jit(solution)/shard_map/all_to_all | solution.py:63
  228.6 0.5 broadcast.144
  229.1 0.7 reduce.9
  229.8 0.1 all_to_all.26
  229.9 0.0 all-reduce.3.cloned.1.call-done
  229.9 0.0 all-reduce.5.cloned.1.call-update
  230.0 83.2 %all-gather.8.cloned.1.call-done = bf16[8192,512]{1,0:T(8,128)(2,1)} async-done(((bf16[1024,512]{1,0:T(8,128)(2,1)}), bf16[8192,512]{1,0:T(8,128)(2,1)}) %all-gather.8.cloned.1.call-update) | async-done | bytes 8388624 | tf_op jit(solution)/shard_map/all_gather | solution.py:37
  313.2 10.2 %convolution_convert_fusion = bf16[512,512]{1,0:T(8,128)(2,1)S(1)} fusion(bf16[512,8192]{1,0:T(8,128)(2,1)} %all-gather.4.cloned.1.call-done, bf16[8192,512]{1,0:T(8,128)(2,1)} %all-gather.8.cloned.1.call-done), kind=kOutput, calls=%fused_computation.5 | convolution fusion | flops 4295229440 | bytes 17301504 | tf_op jit(solution)/shard_map/dot_general | solution.py:35
  323.4 0.3 copy.19
  323.7 2.6 gather_fusion.3
  326.3 3.7 all-to-all-start.2
  330.0 22.9 %all-reduce.5.cloned.1.call-done = f32[4,128,128]{2,1,0:T(8,128)} async-done(((f32[4,128,128]{2,1,0:T(8,128)}), f32[4,128,128]{2,1,0:T(8,128)}) %all-reduce.5.cloned.1.call-update) | async-done | bytes 262160 | tf_op jit(solution)/shard_map/psum | solution.py:14
  352.9 1.1 select_reduce_fusion.1
  354.0 1.0 multiply_add_fusion
  355.0 0.1 copy.21
  355.2 1.1 fusion.3
  356.2 46.9 %custom-call.7 = f32[4,128,128]{2,1,0:T(8,128)S(1)} custom-call(f32[4,128,128]{2,1,0:T(8,128)S(1)} %fusion.3), custom_call_target="Cholesky" | custom-call | tf_op jit(solution)/shard_map/jit(cholesky)/cholesky | solution.py:46
  403.2 0.1 compare_reduce_fusion
  403.3 0.1 select_bitcast_fusion
  403.4 39.3 %custom-call.8 = f32[4,1,128,128]{2,3,1,0:T(8,128)S(1)} custom-call(f32[4,1,128,128]{3,2,1,0:T(8,128)S(1)} %select_bitcast_fusion), custom_call_target="InvertDiagBlocksLowerTriangular" | custom-call | tf_op jit(solution)/shard_map/triangular_solve | solution.py:50
  442.7 0.6 fusion
  443.3 1.3 convolution_convert_fusion.2
  444.6 0.1 copy.24
  444.7 2.6 gather_fusion.1
  447.3 0.0 all-to-all-done.2
  447.3 3.4 all-to-all-start.1
  450.7 3.8 sort.32
  454.5 2.6 gather_fusion.4
  457.2 3.2 all-to-all-done.1
  460.4 2.6 gather_fusion.2
  (16 shorter events, 0.1 us)
Async XLA Ops:
  7.2 436.2 %copy-start = (f32[4,128,64]{1,2,0:T(8,128)S(1)}, f32[4,128,64]{1,2,0:T(8,128)}, u32[]{:S(2)}) copy-start(f32[4,128,64]{1,2,0:T(8,128)} %param.8) | copy-start | bytes 393220
  7.2 109.1 %all-gather.4.cloned.1.call-start = ((), (), s32[]{:S(2)}) async-start(), calls=%async_computation.3 | async-start | bytes 12582912 | tf_op jit(solution)/shard_map/all_gather | solution.py:29
  7.9 192.1 %all-gather.6.cloned.1.call-start = ((), (), s32[]{:S(2)}) async-start(), calls=%async_computation.4 | async-start | bytes 9437184 | tf_op jit(solution)/shard_map/all_gather | solution.py:32
  8.7 203.2 %copy-start.1 = (s32[512]{0:T(512)S(1)}, s32[512]{0:T(512)}, u32[]{:S(2)}) copy-start(s32[512]{0:T(512)} %param.9) | copy-start | bytes 6148
  8.7 221.3 %all-reduce.3.cloned.1.call-start = ((), (), s32[]{:S(2)}) async-start(), calls=%async_computation.5 | async-start | bytes 524288 | tf_op jit(solution)/shard_map/psum | solution.py:14
  211.3 101.8 %all-gather.8.cloned.1.call-start = ((), (), s32[]{:S(2)}) async-start(), calls=%async_computation.7 | async-start | bytes 9437184 | tf_op jit(solution)/shard_map/all_gather | solution.py:37
  219.9 8.7 %all-to-all-start = ((s32[8,64,1]{1,2,0:T(1,128)}), s32[8,64,1]{1,2,0:T(1,128)S(1)}, u32[]{:S(2)}, u32[]{:S(2)}) async-start(s32[8,64,1]{1,2,0:T(1,128)} %bitcast.7), calls=%async_computation | async-start | bytes 8192 | tf_op jit(solution)/shard_map/all_to_all | solution.py:63
  223.2 129.7 %all-reduce.5.cloned.1.call-start = ((), (), s32[]{:S(2)}) async-start(), calls=%async_computation.6 | async-start | bytes 524288 | tf_op jit(solution)/shard_map/psum | solution.py:14
  326.3 121.0 %all-to-all-start.2 = ((bf16[8,64,512]{2,1,0:T(8,128)(2,1)}), bf16[8,64,512]{2,1,0:T(8,128)(2,1)S(1)}, u32[]{:S(2)}, u32[]{:S(2)}) async-start(bf16[8,64,512]{2,1,0:T(8,128)(2,1)} %bitcast.11), calls=%async_computation.2 | async-start | bytes 1048576 | tf_op jit(solution)/shard_map/all_to_all | solution.py:69
  447.3 13.1 %all-to-all-start.1 = ((bf16[8,64,256]{2,1,0:T(8,128)(2,1)}), bf16[8,64,256]{2,1,0:T(8,128)(2,1)S(1)}, u32[]{:S(2)}, u32[]{:S(2)}) async-start(bf16[8,64,256]{2,1,0:T(8,128)(2,1)} %bitcast.9), calls=%async_computation.1 | async-start | bytes 524288 | tf_op jit(solution)/shard_map/all_to_all | solution.py:66
Sparse Core Ops, SparseCore 0:
  9.6 106.6 all-gather.3
  117.9 82.0 all-gather.5
  211.4 16.8 all-reduce.2
  229.9 83.2 all-gather.7
  315.5 37.4 all-reduce.4
